TPU v7x, 512 devices: a whole 4x4x16 slice. The times are simulated.
512 devices in a mesh: dp: 4 (over y), frames: 16 (over z), height: 8 (over x, core).
Axes of the slice: x: 4, y: 4, z: 16, core: 2. Of those that a mesh axis runs over, the one named last changes fastest.
Arguments:
- video: bfloat16 [512, 8, 16, 640], P(('dp', 'frames'), 'height'), parts along dimension 0
- window_gaps: int32 [112], P('dp'), parts along dimension 0, may hold values from 1 to 8, 112 in all
- gn_gain: float32 [640], replicated, may hold values from 0.25 to 1.75
- gn_bias: float32 [640], replicated, may hold values from -3 to 3
- conv_weight: bfloat16 [5760, 640], P('frames', 'height'), may hold values from -0.078125 to 0.078125
- conv_bias: float32 [640], replicated, may hold values from -3 to 3
- ln_gain: float32 [640], replicated, may hold values from 0.25 to 1.75
- ln_bias: float32 [640], replicated, may hold values from -3 to 3
- qkv_weight: bfloat16 [640, 1920], replicated, may hold values from -0.25 to 0.25
- out_weight: bfloat16 [640, 640], replicated, may hold values from -0.5 to 0.5
- out_bias: float32 [640], replicated, may hold values from -3 to 3
Outputs:
- output: bfloat16 [512, 8, 16, 640], P(('dp', 'frames'), 'height'), parts along dimension 0
There are 4 independent parts, one for each index of `dp`. A program takes and returns all parts, laid end to end along the dimension named above; an argument that names none is the same for every part. Nothing has to cross between parts.
Inputs may be any that keep to these rules, and one draw needn't show every extreme that they name: `window_gaps`: the first window starts at frame 0 and the last at 112; the largest gap 16 // 2 is reached in every draw.
All inputs are finite; a program needn't handle non-finite values.
Results may differ from a plain program's by a relative error of at most 0.008.
Values may be sent and summed in bfloat16 or wider, within the bound.
No kernel may reach another device: no remote copies, remote signals or barrier semaphores. Data moves between devices by JAX's collectives and lax.ppermute only.
A program may use at most 64 MiB of HBM per device.

v0:
```python
import jax
import jax.numpy as jnp
from jax import lax
from jax.sharding import PartitionSpec as P

HEADS = 10
GROUPS = 32
WIN = 16
HEAD_DIM = 64
EPSILON = 1e-05


def passed_along(shard, axis, by):
    size = lax.axis_size(axis)
    pairs = [(i, i + by) for i in range(size) if 0 <= i + by < size]
    return lax.ppermute(shard, axis, pairs)


def extended_2(cells, sides, width):
    for axis, dim in sides:
        count = lax.axis_size(axis)
        ends = count - 1
        head = lax.slice_in_dim(cells, 0, width, axis=dim)
        tail = lax.slice_in_dim(cells, cells.shape[dim] - width, cells.shape[dim], axis=dim)
        cells = jnp.concatenate(
            [
                lax.ppermute(tail, axis, [(i, (i + 1) % count) for i in range(ends)]),
                cells,
                lax.ppermute(head, axis, [((i + 1) % count, i) for i in range(ends)]),
            ],
            axis=dim,
        )
    return cells


def fetch_neighbour(keys, values, offset):
    return passed_along((keys, values), "frames", offset)


def window_starts(window_gaps):
    return jnp.concatenate([jnp.zeros((1,), jnp.int32), jnp.cumsum(window_gaps)])


def on_device(
    video,
    window_gaps,
    gn_gain,
    gn_bias,
    conv_weight,
    conv_bias,
    ln_gain,
    ln_bias,
    qkv_weight,
    out_weight,
    out_bias,
):
    frames_dev, rows_dev, width, chans = video.shape
    bands = lax.axis_size("height")
    floats = video.astype(jnp.float32)
    grouped = floats.reshape(frames_dev, rows_dev, width, GROUPS, chans // GROUPS)
    cell_count = rows_dev * bands * width * (chans // GROUPS)
    mean = lax.psum(jnp.sum(grouped, axis=(1, 2, 4)), "height") / cell_count
    centred = grouped - mean[:, None, None, :, None]
    variance = lax.psum(jnp.sum(centred * centred, axis=(1, 2, 4)), "height") / cell_count
    scaled = (grouped - mean[:, None, None, :, None]) * lax.rsqrt(variance + EPSILON)[
        :, None, None, :, None
    ]
    normed = scaled.reshape(floats.shape) * gn_gain + gn_bias
    activated = jax.nn.silu(normed).astype(jnp.bfloat16)
    columns = lax.all_gather(conv_weight, "height", axis=1, tiled=True)
    extended = extended_2(activated, (("height", 1),), 1)
    extended = jnp.pad(extended, ((0, 0), (0, 0), (1, 1), (0, 0)))
    patches = jnp.concatenate(
        [
            extended[:, row_off : row_off + rows_dev, col_off : col_off + width]
            for row_off in range(3)
            for col_off in range(3)
        ],
        axis=3,
    ).reshape(-1, 9 * chans)
    conv_sum = jnp.dot(
        patches,
        lax.all_gather(columns, "frames", axis=0, tiled=True),
        preferred_element_type=jnp.float32,
    )
    conv_out = (
        (conv_sum + conv_bias).astype(jnp.bfloat16).reshape(frames_dev, rows_dev, width, chans)
    )
    conv_out = lax.optimization_barrier(conv_out)
    resid_state = (floats + conv_out.astype(jnp.float32)).astype(jnp.bfloat16)
    resid_float = resid_state.astype(jnp.float32)
    centre = jnp.mean(resid_float, axis=-1, keepdims=True)
    deviation = resid_float - centre
    spread = jnp.mean(deviation * deviation, axis=-1, keepdims=True)
    normalized = (deviation * lax.rsqrt(spread + EPSILON) * ln_gain + ln_bias).astype(jnp.bfloat16)
    cells = rows_dev * width
    project = jnp.dot(
        normalized.reshape(-1, chans), qkv_weight, preferred_element_type=jnp.float32
    ).astype(jnp.bfloat16)
    scale = HEAD_DIM ** (-0.5)
    starts = window_starts(window_gaps)
    project = project.reshape(frames_dev, cells, 3 * chans)
    query = project[:, :, :chans]
    keys = project[:, :, chans : 2 * chans]
    values = project[:, :, 2 * chans :]
    gathered = [fetch_neighbour(keys, values, offset) for offset in (2, 1)]
    gathered.append((keys, values))
    gathered = gathered + [fetch_neighbour(keys, values, offset) for offset in (-1, -2)]
    keys_near = jnp.concatenate([pair[0] for pair in gathered], axis=0).reshape(
        -1, cells, HEADS, HEAD_DIM
    )
    values_near = jnp.concatenate([pair[1] for pair in gathered], axis=0).reshape(
        -1, cells, HEADS, HEAD_DIM
    )
    near_ids = (lax.axis_index("frames") - 2) * frames_dev + jnp.arange(
        5 * frames_dev, dtype=jnp.int32
    )
    inside = (near_ids[None, :] >= starts[:, None]) & (near_ids[None, :] < starts[:, None] + WIN)
    member = inside.astype(jnp.float32)
    cover = member[:, 2 * frames_dev : 3 * frames_dev].T
    frame_count = jnp.sum(cover, axis=1)
    scores = (
        jnp.einsum(
            "nshd,mshd->shnm",
            query.reshape(frames_dev, cells, HEADS, HEAD_DIM),
            keys_near,
            preferred_element_type=jnp.float32,
        )
        * scale
    )
    expo = jnp.exp(scores)
    window_sum = jnp.einsum("shnm,wm->shnw", expo, member, precision=lax.Precision.HIGHEST)
    coef = cover / (frame_count[:, None] * jnp.where(cover > 0, window_sum, 1.0))
    spread_back = jnp.einsum("shnw,wm->shnm", coef, member, precision=lax.Precision.HIGHEST)
    attn_weight = (expo * spread_back).astype(jnp.bfloat16)
    mixed = (
        jnp.einsum("shnm,mshd->nshd", attn_weight, values_near, preferred_element_type=jnp.float32)
        .astype(jnp.bfloat16)
        .reshape(-1, chans)
    )
    projected = jnp.dot(mixed, out_weight, preferred_element_type=jnp.float32)
    output = resid_float.reshape(-1, chans) + projected + out_bias
    return output.astype(jnp.bfloat16).reshape(frames_dev, rows_dev, width, chans)


def solution(mesh):
    placed = (
        P(("dp", "frames"), "height", None, None),
        P("dp"),
        P(),
        P(),
        P("frames", "height"),
        P(),
        P(),
        P(),
        P(),
        P(),
        P(),
    )
    return jax.shard_map(
        on_device,
        mesh=mesh,
        in_specs=placed,
        out_specs=P(("dp", "frames"), "height", None, None),
        check_vma=False,
    )
```

profile of v0, /device:TPU:2, one launch (start us, length us, event | category | flops | bytes accessed | tf_op | source)
XLA Modules:
  0.0 188.5 jit_solution(935710017307930549)
XLA Ops:
  6.5 16.2 %all_gather.6 = bf16[360,640]{0,1:T(8,128)(2,1)S(1)} all-gather(bf16[360,80]{0,1:T(8,128)(2,1)} %param.15), channel_id=1, replica_groups=mesh['dp'=4,'frames'=16,'height'=8] {'height'}, dimensions={1}, use_global_device_ids=true | all-gather | bytes 518400 | tf_op jit(solution)/shard_map/all_gather | solution.py:70
  22.7 1.0 copy.46
  24.2 13.0 %psum.14 = f32[8,32]{1,0:T(8,128)S(1)} all-reduce(f32[8,32]{1,0:T(8,128)S(1)} %reduce_sum.61), channel_id=1, replica_groups=mesh['dp'=4,'frames'=16,'height'=8] {'height'}, use_global_device_ids=true, to_apply=%region_2.0 | all-reduce | flops 256 | bytes 2048 | tf_op jit(solution)/shard_map/psum | solution.py:62
  37.8 12.3 %psum.15 = f32[8,32]{1,0:T(8,128)S(1)} all-reduce(f32[8,32]{1,0:T(8,128)S(1)} %reduce_sum.64), channel_id=1, replica_groups=mesh['dp'=4,'frames'=16,'height'=8] {'height'}, use_global_device_ids=true, to_apply=%region_5.6 | all-reduce | flops 256 | bytes 2048 | tf_op jit(solution)/shard_map/psum | solution.py:64
  50.5 1.9 %collective-permute-start = (bf16[8,1,16,640]{3,2,1,0:T(8,128)(2,1)S(1)}, bf16[8,1,16,640]{3,2,1,0:T(8,128)(2,1)S(1)}, u32[]{:S(2)}, u32[]{:S(2)}) collective-permute-start(bf16[8,1,16,640]{3,2,1,0:T(8,128)(2,1)S(1)} %fusion.38), channel_id=1, source_target_pairs={{0,1},{1,2},{2,3},{3,4},{4,5},{5,6},{6,7},{8,9},{9,10},{10,11},{11... | collective-permute-start | bytes 491528 | tf_op jit(solution)/shard_map/ppermute | solution.py:27
  52.4 4.7 %collective-permute-start.1 = (bf16[8,1,16,640]{3,2,1,0:T(8,128)(2,1)S(1)}, bf16[8,1,16,640]{3,2,1,0:T(8,128)(2,1)S(1)}, u32[]{:S(2)}, u32[]{:S(2)}) collective-permute-start(bf16[8,1,16,640]{3,2,1,0:T(8,128)(2,1)S(1)} %fusion.38), channel_id=1, source_target_pairs={{1,0},{2,1},{3,2},{4,3},{5,4},{6,5},{7,6},{9,8},{10,9},{11,10},{12... | collective-permute-start | bytes 491528 | tf_op jit(solution)/shard_map/ppermute | solution.py:29
  58.2 1.8 collective-permute-done.1
  61.6 0.7 slice_dynamic-update-slice_fusion.4
  63.1 0.8 constant_dynamic-update-slice_fusion.1
  63.9 0.8 slice_dynamic-update-slice_fusion.2
  66.0 0.8 slice_dynamic-update-slice_fusion
  66.7 54.3 %all-gather.2.cloned.1.call-done = bf16[5760,640]{1,0:T(8,128)(2,1)} async-done(((bf16[360,640]{1,0:T(8,128)(2,1)}), bf16[5760,640]{1,0:T(8,128)(2,1)}) %all-gather.2.cloned.1.call-update) | async-done | bytes 7372816 | tf_op jit(solution)/shard_map/all_gather | solution.py:83
  121.0 4.9 %fusion.21 = bf16[128,640]{1,0:T(8,128)(2,1)S(1)} fusion(bf16[128,5760]{1,0:T(8,128)(2,1)} %bitcast, bf16[5760,640]{1,0:T(8,128)(2,1)} %all-gather.2.cloned.1.call-done, f32[640]{0:T(1024)S(1)} %copy-done.6), kind=kOutput, calls=%fused_computation.20 | convolution fusion | flops 943882240 | bytes 9013760 | tf_op jit(solution)/shard_map/dot_general | solution.py:81
  127.1 2.7 %collective-permute-start.6 = (bf16[8,16,640]{2,1,0:T(8,128)(2,1)S(1)}, bf16[8,16,640]{2,1,0:T(8,128)(2,1)S(1)}, u32[]{:S(2)}, u32[]{:S(2)}) collective-permute-start(bf16[8,16,640]{2,1,0:T(8,128)(2,1)S(1)} %get-tuple-element.11), channel_id=1, source_target_pairs={{0,16},{8,24},{16,32},{24,40},{32,48},{40,56},{48,64},{56,72},{64,... | collective-permute-start | bytes 491528 | tf_op jit(solution)/shard_map/ppermute | solution.py:16
  129.8 4.9 %collective-permute-start.2 = (bf16[8,16,640]{2,1,0:T(8,128)(2,1)S(1)}, bf16[8,16,640]{2,1,0:T(8,128)(2,1)S(1)}, u32[]{:S(2)}, u32[]{:S(2)}) collective-permute-start(bf16[8,16,640]{2,1,0:T(8,128)(2,1)S(1)} %get-tuple-element.10), channel_id=1, source_target_pairs={{0,16},{8,24},{16,32},{24,40},{32,48},{40,56},{48,64},{56,72},{64,... | collective-permute-start | bytes 491528 | tf_op jit(solution)/shard_map/ppermute | solution.py:16
  134.8 3.8 %collective-permute-start.7 = (bf16[8,16,640]{2,1,0:T(8,128)(2,1)S(1)}, bf16[8,16,640]{2,1,0:T(8,128)(2,1)S(1)}, u32[]{:S(2)}, u32[]{:S(2)}) collective-permute-start(bf16[8,16,640]{2,1,0:T(8,128)(2,1)S(1)} %get-tuple-element.11), channel_id=1, source_target_pairs={{0,8},{8,16},{16,24},{24,32},{32,40},{40,48},{48,56},{56,64},{64,7... | collective-permute-start | bytes 491528 | tf_op jit(solution)/shard_map/ppermute | solution.py:16
  138.6 3.8 %collective-permute-start.3 = (bf16[8,16,640]{2,1,0:T(8,128)(2,1)S(1)}, bf16[8,16,640]{2,1,0:T(8,128)(2,1)S(1)}, u32[]{:S(2)}, u32[]{:S(2)}) collective-permute-start(bf16[8,16,640]{2,1,0:T(8,128)(2,1)S(1)} %get-tuple-element.10), channel_id=1, source_target_pairs={{0,8},{8,16},{16,24},{24,32},{32,40},{40,48},{48,56},{56,64},{64,7... | collective-permute-start | bytes 491528 | tf_op jit(solution)/shard_map/ppermute | solution.py:16
  142.4 1.3 collective-permute-start.4
  143.7 1.3 collective-permute-start.5
  145.0 1.3 collective-permute-start.8
  147.0 1.3 collective-permute-start.9
  149.0 0.7 constant_dynamic-update-slice_fusion.5
  149.7 0.9 copy-done.3
  150.6 0.9 collective-permute-done.4
  152.2 7.9 %collective-permute-done.5 = bf16[8,16,640]{2,1,0:T(8,128)(2,1)S(1)} collective-permute-done((bf16[8,16,640]{2,1,0:T(8,128)(2,1)S(1)}, bf16[8,16,640]{2,1,0:T(8,128)(2,1)S(1)}, u32[]{:S(2)}, u32[]{:S(2)}) %collective-permute-start.5) | collective-permute-done | bytes 163872 | tf_op jit(solution)/shard_map/ppermute | solution.py:16
  160.8 4.1 %reshape.144 = bf16[40,16,10,64]{3,2,1,0:T(8,128)(2,1)} reshape(bf16[40,16,640]{2,1,0:T(8,128)(2,1)} %constant_dynamic-update-slice_fusion.3) | data formatting | bytes 1638400 | tf_op jit(solution)/shard_map/reshape | solution.py:112
  165.6 2.7 %collective-permute-done.9 = bf16[8,16,640]{2,1,0:T(8,128)(2,1)S(1)} collective-permute-done((bf16[8,16,640]{2,1,0:T(8,128)(2,1)S(1)}, bf16[8,16,640]{2,1,0:T(8,128)(2,1)S(1)}, u32[]{:S(2)}, u32[]{:S(2)}) %collective-permute-start.9) | collective-permute-done | bytes 163872 | tf_op jit(solution)/shard_map/ppermute | solution.py:16
  168.9 4.1 %reshape.146 = bf16[40,16,10,64]{3,2,1,0:T(8,128)(2,1)} reshape(bf16[40,16,640]{2,1,0:T(8,128)(2,1)} %constant_dynamic-update-slice_fusion.8) | data formatting | bytes 1638400 | tf_op jit(solution)/shard_map/reshape | solution.py:109
  173.3 3.0 %fusion.8 = f32[16,10,8,40]{3,2,1,0:T(8,128)S(1)} fusion(bf16[40,16,10,64]{3,2,1,0:T(8,128)(2,1)} %reshape.146, bf16[8,16,10,64]{3,2,1,0:T(8,128)(2,1)S(1)} %reshape.145), kind=kOutput, calls=%fused_computation.10 | convolution fusion | flops 6604800 | bytes 1187840 | tf_op jit(solution)/shard_map/nshd,mshd->shnm/dot_general | solution.py:123
  177.3 0.7 copy-done.2
  178.0 1.0 fusion.18
  179.5 2.1 %fusion.22 = bf16[128,640]{1,0:T(8,128)(2,1)} fusion(bf16[128,640]{1,0:T(8,128)(2,1)S(1)} %reshape.149, bf16[640,640]{1,0:T(8,128)(2,1)} %param.20, f32[640]{0:T(1024)S(1)} %copy-done.9, bf16[128,640]{1,0:T(8,128)(2,1)S(1)} %bitcast.36), kind=kOutput, calls=%fused_computation.21 | convolution fusion | flops 105185280 | bytes 1313280 | tf_op jit(solution)/shard_map/dot_general | solution.py:141
  (76 shorter events, 13.0 us)
Async XLA Ops:
  6.5 119.9 %copy-start = (bf16[640,1920]{1,0:T(8,128)(2,1)S(1)}, bf16[640,1920]{1,0:T(8,128)(2,1)}, u32[]{:S(2)}) copy-start(bf16[640,1920]{1,0:T(8,128)(2,1)} %param.19) | copy-start | bytes 7372804
  6.5 17.3 %copy-start.1 = (bf16[8,1,16,640]{3,2,1,0:T(8,128)(2,1)S(1)}, bf16[8,1,16,640]{3,2,1,0:T(8,128)(2,1)}, u32[]{:S(2)}) copy-start(bf16[8,1,16,640]{3,2,1,0:T(8,128)(2,1)} %param.11) | copy-start | bytes 491524
  6.5 114.5 %all-gather.2.cloned.1.call-start = ((), (), s32[]{:S(2)}) async-start(), calls=%async_computation | async-start | bytes 7833600 | tf_op jit(solution)/shard_map/all_gather | solution.py:83
  22.7 27.6 %copy-start.4 = (f32[640]{0:T(1024)S(1)}, f32[640]{0:T(1024)}, u32[]{:S(2)}) copy-start(f32[640]{0:T(1024)} %param.14) | copy-start | bytes 7684
  22.7 27.6 %copy-start.5 = (f32[640]{0:T(1024)S(1)}, f32[640]{0:T(1024)}, u32[]{:S(2)}) copy-start(f32[640]{0:T(1024)} %param.13) | copy-start | bytes 7684
  22.7 34.4 %copy-start.10 = (s32[28]{0:T(128)S(1)}, s32[28]{0:T(128)}, u32[]{:S(2)}) copy-start(s32[28]{0:T(128)} %param.12) | copy-start | bytes 340
  50.5 7.7 %collective-permute-start = (bf16[8,1,16,640]{3,2,1,0:T(8,128)(2,1)S(1)}, bf16[8,1,16,640]{3,2,1,0:T(8,128)(2,1)S(1)}, u32[]{:S(2)}, u32[]{:S(2)}) collective-permute-start(bf16[8,1,16,640]{3,2,1,0:T(8,128)(2,1)S(1)} %fusion.38), channel_id=1, source_target_pairs={{0,1},{1,2},{2,3},{3,4},{4,5},{5,6},{6,7},{8,9},{9,10},{10,11},{11... | collective-permute-start | bytes 491528 | tf_op jit(solution)/shard_map/ppermute | solution.py:27
  52.4 7.5 %collective-permute-start.1 = (bf16[8,1,16,640]{3,2,1,0:T(8,128)(2,1)S(1)}, bf16[8,1,16,640]{3,2,1,0:T(8,128)(2,1)S(1)}, u32[]{:S(2)}, u32[]{:S(2)}) collective-permute-start(bf16[8,1,16,640]{3,2,1,0:T(8,128)(2,1)S(1)} %fusion.38), channel_id=1, source_target_pairs={{1,0},{2,1},{3,2},{4,3},{5,4},{6,5},{7,6},{9,8},{10,9},{11,10},{12... | collective-permute-start | bytes 491528 | tf_op jit(solution)/shard_map/ppermute | solution.py:29
  60.2 60.8 %copy-start.6 = (f32[640]{0:T(1024)S(1)}, f32[640]{0:T(1024)}, u32[]{:S(2)}) copy-start(f32[640]{0:T(1024)} %param.16) | copy-start | bytes 7684
  121.0 5.3 %copy-start.7 = (f32[640]{0:T(1024)S(1)}, f32[640]{0:T(1024)}, u32[]{:S(2)}) copy-start(f32[640]{0:T(1024)} %param.18) | copy-start | bytes 7684
  121.0 5.3 %copy-start.8 = (f32[640]{0:T(1024)S(1)}, f32[640]{0:T(1024)}, u32[]{:S(2)}) copy-start(f32[640]{0:T(1024)} %param.17) | copy-start | bytes 7684
  127.1 16.6 %collective-permute-start.6 = (bf16[8,16,640]{2,1,0:T(8,128)(2,1)S(1)}, bf16[8,16,640]{2,1,0:T(8,128)(2,1)S(1)}, u32[]{:S(2)}, u32[]{:S(2)}) collective-permute-start(bf16[8,16,640]{2,1,0:T(8,128)(2,1)S(1)} %get-tuple-element.11), channel_id=1, source_target_pairs={{0,16},{8,24},{16,32},{24,40},{32,48},{40,56},{48,64},{56,72},{64,... | collective-permute-start | bytes 491528 | tf_op jit(solution)/shard_map/ppermute | solution.py:16
  129.8 15.2 %collective-permute-start.2 = (bf16[8,16,640]{2,1,0:T(8,128)(2,1)S(1)}, bf16[8,16,640]{2,1,0:T(8,128)(2,1)S(1)}, u32[]{:S(2)}, u32[]{:S(2)}) collective-permute-start(bf16[8,16,640]{2,1,0:T(8,128)(2,1)S(1)} %get-tuple-element.10), channel_id=1, source_target_pairs={{0,16},{8,24},{16,32},{24,40},{32,48},{40,56},{48,64},{56,72},{64,... | collective-permute-start | bytes 491528 | tf_op jit(solution)/shard_map/ppermute | solution.py:16
  134.8 12.2 %collective-permute-start.7 = (bf16[8,16,640]{2,1,0:T(8,128)(2,1)S(1)}, bf16[8,16,640]{2,1,0:T(8,128)(2,1)S(1)}, u32[]{:S(2)}, u32[]{:S(2)}) collective-permute-start(bf16[8,16,640]{2,1,0:T(8,128)(2,1)S(1)} %get-tuple-element.11), channel_id=1, source_target_pairs={{0,8},{8,16},{16,24},{24,32},{32,40},{40,48},{48,56},{56,64},{64,7... | collective-permute-start | bytes 491528 | tf_op jit(solution)/shard_map/ppermute | solution.py:16
  138.6 9.7 %collective-permute-start.3 = (bf16[8,16,640]{2,1,0:T(8,128)(2,1)S(1)}, bf16[8,16,640]{2,1,0:T(8,128)(2,1)S(1)}, u32[]{:S(2)}, u32[]{:S(2)}) collective-permute-start(bf16[8,16,640]{2,1,0:T(8,128)(2,1)S(1)} %get-tuple-element.10), channel_id=1, source_target_pairs={{0,8},{8,16},{16,24},{24,32},{32,40},{40,48},{48,56},{56,64},{64,7... | collective-permute-start | bytes 491528 | tf_op jit(solution)/shard_map/ppermute | solution.py:16
  142.4 9.1 %collective-permute-start.4 = (bf16[8,16,640]{2,1,0:T(8,128)(2,1)S(1)}, bf16[8,16,640]{2,1,0:T(8,128)(2,1)S(1)}, u32[]{:S(2)}, u32[]{:S(2)}) collective-permute-start(bf16[8,16,640]{2,1,0:T(8,128)(2,1)S(1)} %get-tuple-element.10), channel_id=1, source_target_pairs={{8,0},{16,8},{24,16},{32,24},{40,32},{48,40},{56,48},{64,56},{72,6... | collective-permute-start | bytes 491528 | tf_op jit(solution)/shard_map/ppermute | solution.py:16
  143.7 16.5 %collective-permute-start.5 = (bf16[8,16,640]{2,1,0:T(8,128)(2,1)S(1)}, bf16[8,16,640]{2,1,0:T(8,128)(2,1)S(1)}, u32[]{:S(2)}, u32[]{:S(2)}) collective-permute-start(bf16[8,16,640]{2,1,0:T(8,128)(2,1)S(1)} %get-tuple-element.10), channel_id=1, source_target_pairs={{16,0},{24,8},{32,16},{40,24},{48,32},{56,40},{64,48},{72,56},{80,... | collective-permute-start | bytes 491528 | tf_op jit(solution)/shard_map/ppermute | solution.py:16
  145.0 19.9 %collective-permute-start.8 = (bf16[8,16,640]{2,1,0:T(8,128)(2,1)S(1)}, bf16[8,16,640]{2,1,0:T(8,128)(2,1)S(1)}, u32[]{:S(2)}, u32[]{:S(2)}) collective-permute-start(bf16[8,16,640]{2,1,0:T(8,128)(2,1)S(1)} %get-tuple-element.11), channel_id=1, source_target_pairs={{8,0},{16,8},{24,16},{32,24},{40,32},{48,40},{56,48},{64,56},{72,6... | collective-permute-start | bytes 491528 | tf_op jit(solution)/shard_map/ppermute | solution.py:16
  147.0 21.3 %collective-permute-start.9 = (bf16[8,16,640]{2,1,0:T(8,128)(2,1)S(1)}, bf16[8,16,640]{2,1,0:T(8,128)(2,1)S(1)}, u32[]{:S(2)}, u32[]{:S(2)}) collective-permute-start(bf16[8,16,640]{2,1,0:T(8,128)(2,1)S(1)} %get-tuple-element.11), channel_id=1, source_target_pairs={{16,0},{24,8},{32,16},{40,24},{48,32},{56,40},{64,48},{72,56},{80,... | collective-permute-start | bytes 491528 | tf_op jit(solution)/shard_map/ppermute | solution.py:16
  149.7 0.9 copy-start.3
  176.3 1.8 copy-start.2
  178.0 1.5 copy-start.9
Sparse Core Ops, SparseCore 0:
  23.9 97.0 all-gather.1
where the time goes:
time: 189 us; the launch traced here: 188 us
  waiting for transfers between devices  68.2 us (36%)
  blocking collectives  41.6 us (22%)
  starting transfers between devices  26.9 us (14%)
  local copies, waits for them, and re-layouts  23 us (12%)
  between operations  13.8 us (7%)
  matrix products  12.6 us (7%)
  other arithmetic  2.48 us (1%)
    all_gather x1, waiting for transfers between devices, on_device(): lax.all_gather(columns, 'frames', axis=0, tiled=True)  54.3 us
    ppermute x8, starting transfers between devices, passed_along(): return lax.ppermute(shard, axis, pairs)  20.3 us
    all_gather x1, blocking collectives, on_device(): columns = lax.all_gather(conv_weight, 'height', axis=1, tiled=True)  16.2 us
    psum x1, blocking collectives, on_device(): mean = lax.psum(jnp.sum(grouped, axis=(1, 2, 4)), 'height') / cell_count  13 us
    psum x1, blocking collectives, on_device(): lax.psum(jnp.sum(centred * centred, axis=(1, 2, 4)), 'height') / cell_count  12.3 us
    ppermute x8, waiting for transfers between devices, passed_along(): return lax.ppermute(shard, axis, pairs)  11.5 us
    unnamed x36, local copies, waits for them, and re-layouts  10.1 us
    dot_general x1, matrix products, on_device(): jnp.dot(patches, lax.all_gather(columns, 'frames', axis=0, tiled=True), p...  4.9 us
  transfers between devices with their start and end apart: 11, of which 6 were waited for; matrix products, arithmetic and copies ran while one was open for 9% of the time, Pallas kernels for 0%

commit v1 on v0

--- a/solution.py
+++ b/solution.py
@@ -59,7 +59,7 @@
     floats = video.astype(jnp.float32)
     grouped = floats.reshape(frames_dev, rows_dev, width, GROUPS, chans // GROUPS)
     cell_count = rows_dev * bands * width * (chans // GROUPS)
-    mean = lax.psum(jnp.sum(grouped, axis=(1, 2, 4)), "height") / cell_count
+    mean = jnp.sum(lax.all_gather(jnp.sum(grouped, axis=(1, 2, 4)), "height"), axis=0) / cell_count
     centred = grouped - mean[:, None, None, :, None]
     variance = lax.psum(jnp.sum(centred * centred, axis=(1, 2, 4)), "height") / cell_count
     scaled = (grouped - mean[:, None, None, :, None]) * lax.rsqrt(variance + EPSILON)[

time: 189 us -> 189 us (level)
    all_gather x0 -> x1, blocking collectives: none -> 13.1 us  [on_device(): lax.all_gather(jnp.sum(grouped, axis=(1, 2, 4)), 'height')]
    psum x1 -> x0, blocking collectives: 13 us -> none  [on_device(): mean = lax.psum(jnp.sum(grouped, axis=(1, 2, 4)), 'height') / cell_count]
where the time goes in v1:
time: 189 us; the launch traced here: 188 us
  waiting for transfers between devices  67.8 us (36%)
  blocking collectives  42.9 us (23%)
  starting transfers between devices  25.9 us (14%)
  local copies, waits for them, and re-layouts  23 us (12%)
  between operations  13.8 us (7%)
  matrix products  12.6 us (7%)
  other arithmetic  2.5 us (1%)
    all_gather x1, waiting for transfers between devices, on_device(): lax.all_gather(columns, 'frames', axis=0, tiled=True)  54 us
    ppermute x8, starting transfers between devices, passed_along(): return lax.ppermute(shard, axis, pairs)  20.3 us
    all_gather x1, blocking collectives, on_device(): columns = lax.all_gather(conv_weight, 'height', axis=1, tiled=True)  16.2 us
    psum x1, blocking collectives, on_device(): lax.psum(jnp.sum(centred * centred, axis=(1, 2, 4)), 'height') / cell_count  13.7 us
    all_gather x1, blocking collectives, on_device(): lax.all_gather(jnp.sum(grouped, axis=(1, 2, 4)), 'height')  13.1 us
    ppermute x8, waiting for transfers between devices, passed_along(): return lax.ppermute(shard, axis, pairs)  11.5 us
    unnamed x36, local copies, waits for them, and re-layouts  10.1 us
    dot_general x1, matrix products, on_device(): jnp.dot(patches, lax.all_gather(columns, 'frames', axis=0, tiled=True), p...  4.9 us
  transfers between devices with their start and end apart: 11, of which 6 were waited for; matrix products, arithmetic and copies ran while one was open for 9% of the time, Pallas kernels for 0%

profile of v1, /device:TPU:2, one launch (start us, length us, event | category | flops | bytes accessed | tf_op | source)
XLA Modules:
  0.0 188.5 jit_solution(1370518906052033242)
XLA Ops:
  6.5 16.2 %all_gather.14 = bf16[360,640]{0,1:T(8,128)(2,1)S(1)} all-gather(bf16[360,80]{0,1:T(8,128)(2,1)} %param.15), channel_id=1, replica_groups=mesh['dp'=4,'frames'=16,'height'=8] {'height'}, dimensions={1}, use_global_device_ids=true | all-gather | bytes 518400 | tf_op jit(solution)/shard_map/all_gather | solution.py:70
  22.7 1.0 copy.56
  24.2 13.1 %all-gather = f32[64,32]{1,0:T(8,128)S(1)} all-gather(f32[8,32]{1,0:T(8,128)S(1)} %reduce_sum.70), channel_id=2, replica_groups=mesh['dp'=4,'frames'=16,'height'=8] {'height'}, dimensions={0}, use_global_device_ids=true | all-gather | bytes 9216 | tf_op jit(solution)/shard_map/all_gather | solution.py:62
  37.8 13.7 %psum.7 = f32[8,32]{1,0:T(8,128)S(1)} all-reduce(f32[8,32]{1,0:T(8,128)S(1)} %reduce_sum.74), channel_id=1, replica_groups=mesh['dp'=4,'frames'=16,'height'=8] {'height'}, use_global_device_ids=true, to_apply=%region_5.6 | all-reduce | flops 256 | bytes 2048 | tf_op jit(solution)/shard_map/psum | solution.py:64
  51.9 1.9 %collective-permute-start = (bf16[8,1,16,640]{3,2,1,0:T(8,128)(2,1)S(1)}, bf16[8,1,16,640]{3,2,1,0:T(8,128)(2,1)S(1)}, u32[]{:S(2)}, u32[]{:S(2)}) collective-permute-start(bf16[8,1,16,640]{3,2,1,0:T(8,128)(2,1)S(1)} %fusion.38), channel_id=1, source_target_pairs={{0,1},{1,2},{2,3},{3,4},{4,5},{5,6},{6,7},{8,9},{9,10},{10,11},{11... | collective-permute-start | bytes 491528 | tf_op jit(solution)/shard_map/ppermute | solution.py:27
  53.8 3.6 %collective-permute-start.1 = (bf16[8,1,16,640]{3,2,1,0:T(8,128)(2,1)S(1)}, bf16[8,1,16,640]{3,2,1,0:T(8,128)(2,1)S(1)}, u32[]{:S(2)}, u32[]{:S(2)}) collective-permute-start(bf16[8,1,16,640]{3,2,1,0:T(8,128)(2,1)S(1)} %fusion.38), channel_id=1, source_target_pairs={{1,0},{2,1},{3,2},{4,3},{5,4},{6,5},{7,6},{9,8},{10,9},{11,10},{12... | collective-permute-start | bytes 491528 | tf_op jit(solution)/shard_map/ppermute | solution.py:29
  58.5 1.8 collective-permute-done.1
  61.9 0.7 slice_dynamic-update-slice_fusion.4
  63.4 0.8 constant_dynamic-update-slice_fusion.1
  64.2 0.8 slice_dynamic-update-slice_fusion.2
  66.3 0.8 slice_dynamic-update-slice_fusion
  67.1 54.0 %all-gather.3.cloned.1.call-done = bf16[5760,640]{1,0:T(8,128)(2,1)} async-done(((bf16[360,640]{1,0:T(8,128)(2,1)}), bf16[5760,640]{1,0:T(8,128)(2,1)}) %all-gather.3.cloned.1.call-update) | async-done | bytes 7372816 | tf_op jit(solution)/shard_map/all_gather | solution.py:83
  121.0 4.9 %fusion.21 = bf16[128,640]{1,0:T(8,128)(2,1)S(1)} fusion(bf16[128,5760]{1,0:T(8,128)(2,1)} %bitcast.1, bf16[5760,640]{1,0:T(8,128)(2,1)} %all-gather.3.cloned.1.call-done, f32[640]{0:T(1024)S(1)} %copy-done.6), kind=kOutput, calls=%fused_computation.20 | convolution fusion | flops 943882240 | bytes 9013760 | tf_op jit(solution)/shard_map/dot_general | solution.py:81
  127.1 2.7 %collective-permute-start.6 = (bf16[8,16,640]{2,1,0:T(8,128)(2,1)S(1)}, bf16[8,16,640]{2,1,0:T(8,128)(2,1)S(1)}, u32[]{:S(2)}, u32[]{:S(2)}) collective-permute-start(bf16[8,16,640]{2,1,0:T(8,128)(2,1)S(1)} %get-tuple-element.11), channel_id=1, source_target_pairs={{0,16},{8,24},{16,32},{24,40},{32,48},{40,56},{48,64},{56,72},{64,... | collective-permute-start | bytes 491528 | tf_op jit(solution)/shard_map/ppermute | solution.py:16
  129.8 4.9 %collective-permute-start.2 = (bf16[8,16,640]{2,1,0:T(8,128)(2,1)S(1)}, bf16[8,16,640]{2,1,0:T(8,128)(2,1)S(1)}, u32[]{:S(2)}, u32[]{:S(2)}) collective-permute-start(bf16[8,16,640]{2,1,0:T(8,128)(2,1)S(1)} %get-tuple-element.10), channel_id=1, source_target_pairs={{0,16},{8,24},{16,32},{24,40},{32,48},{40,56},{48,64},{56,72},{64,... | collective-permute-start | bytes 491528 | tf_op jit(solution)/shard_map/ppermute | solution.py:16
  134.8 3.8 %collective-permute-start.7 = (bf16[8,16,640]{2,1,0:T(8,128)(2,1)S(1)}, bf16[8,16,640]{2,1,0:T(8,128)(2,1)S(1)}, u32[]{:S(2)}, u32[]{:S(2)}) collective-permute-start(bf16[8,16,640]{2,1,0:T(8,128)(2,1)S(1)} %get-tuple-element.11), channel_id=1, source_target_pairs={{0,8},{8,16},{16,24},{24,32},{32,40},{40,48},{48,56},{56,64},{64,7... | collective-permute-start | bytes 491528 | tf_op jit(solution)/shard_map/ppermute | solution.py:16
  138.6 3.8 %collective-permute-start.3 = (bf16[8,16,640]{2,1,0:T(8,128)(2,1)S(1)}, bf16[8,16,640]{2,1,0:T(8,128)(2,1)S(1)}, u32[]{:S(2)}, u32[]{:S(2)}) collective-permute-start(bf16[8,16,640]{2,1,0:T(8,128)(2,1)S(1)} %get-tuple-element.10), channel_id=1, source_target_pairs={{0,8},{8,16},{16,24},{24,32},{32,40},{40,48},{48,56},{56,64},{64,7... | collective-permute-start | bytes 491528 | tf_op jit(solution)/shard_map/ppermute | solution.py:16
  142.4 1.3 collective-permute-start.4
  143.7 1.3 collective-permute-start.5
  145.0 1.3 collective-permute-start.8
  147.0 1.3 collective-permute-start.9
  149.0 0.7 constant_dynamic-update-slice_fusion.5
  149.7 0.9 copy-done.3
  150.6 0.9 collective-permute-done.4
  152.2 7.9 %collective-permute-done.5 = bf16[8,16,640]{2,1,0:T(8,128)(2,1)S(1)} collective-permute-done((bf16[8,16,640]{2,1,0:T(8,128)(2,1)S(1)}, bf16[8,16,640]{2,1,0:T(8,128)(2,1)S(1)}, u32[]{:S(2)}, u32[]{:S(2)}) %collective-permute-start.5) | collective-permute-done | bytes 163872 | tf_op jit(solution)/shard_map/ppermute | solution.py:16
  160.8 4.1 %reshape.146 = bf16[40,16,10,64]{3,2,1,0:T(8,128)(2,1)} reshape(bf16[40,16,640]{2,1,0:T(8,128)(2,1)} %constant_dynamic-update-slice_fusion.3) | data formatting | bytes 1638400 | tf_op jit(solution)/shard_map/reshape | solution.py:112
  165.6 2.7 %collective-permute-done.9 = bf16[8,16,640]{2,1,0:T(8,128)(2,1)S(1)} collective-permute-done((bf16[8,16,640]{2,1,0:T(8,128)(2,1)S(1)}, bf16[8,16,640]{2,1,0:T(8,128)(2,1)S(1)}, u32[]{:S(2)}, u32[]{:S(2)}) %collective-permute-start.9) | collective-permute-done | bytes 163872 | tf_op jit(solution)/shard_map/ppermute | solution.py:16
  168.9 4.1 %reshape.148 = bf16[40,16,10,64]{3,2,1,0:T(8,128)(2,1)} reshape(bf16[40,16,640]{2,1,0:T(8,128)(2,1)} %constant_dynamic-update-slice_fusion.8) | data formatting | bytes 1638400 | tf_op jit(solution)/shard_map/reshape | solution.py:109
  173.3 3.0 %fusion.8 = f32[16,10,8,40]{3,2,1,0:T(8,128)S(1)} fusion(bf16[40,16,10,64]{3,2,1,0:T(8,128)(2,1)} %reshape.148, bf16[8,16,10,64]{3,2,1,0:T(8,128)(2,1)S(1)} %reshape.147), kind=kOutput, calls=%fused_computation.10 | convolution fusion | flops 6604800 | bytes 1187840 | tf_op jit(solution)/shard_map/nshd,mshd->shnm/dot_general | solution.py:123
  177.3 0.7 copy-done.2
  178.0 1.0 fusion.18
  179.5 2.1 %fusion.22 = bf16[128,640]{1,0:T(8,128)(2,1)} fusion(bf16[128,640]{1,0:T(8,128)(2,1)S(1)} %reshape.151, bf16[640,640]{1,0:T(8,128)(2,1)} %param.20, f32[640]{0:T(1024)S(1)} %copy-done.9, bf16[128,640]{1,0:T(8,128)(2,1)S(1)} %bitcast.38), kind=kOutput, calls=%fused_computation.21 | convolution fusion | flops 105185280 | bytes 1313280 | tf_op jit(solution)/shard_map/dot_general | solution.py:141
  (77 shorter events, 13.0 us)
Async XLA Ops:
  6.5 119.9 %copy-start = (bf16[640,1920]{1,0:T(8,128)(2,1)S(1)}, bf16[640,1920]{1,0:T(8,128)(2,1)}, u32[]{:S(2)}) copy-start(bf16[640,1920]{1,0:T(8,128)(2,1)} %param.19) | copy-start | bytes 7372804
  6.5 17.3 %copy-start.1 = (bf16[8,1,16,640]{3,2,1,0:T(8,128)(2,1)S(1)}, bf16[8,1,16,640]{3,2,1,0:T(8,128)(2,1)}, u32[]{:S(2)}) copy-start(bf16[8,1,16,640]{3,2,1,0:T(8,128)(2,1)} %param.11) | copy-start | bytes 491524
  6.5 114.5 %all-gather.3.cloned.1.call-start = ((), (), s32[]{:S(2)}) async-start(), calls=%async_computation | async-start | bytes 7833600 | tf_op jit(solution)/shard_map/all_gather | solution.py:83
  22.7 29.0 %copy-start.4 = (f32[640]{0:T(1024)S(1)}, f32[640]{0:T(1024)}, u32[]{:S(2)}) copy-start(f32[640]{0:T(1024)} %param.14) | copy-start | bytes 7684
  22.7 29.0 %copy-start.5 = (f32[640]{0:T(1024)S(1)}, f32[640]{0:T(1024)}, u32[]{:S(2)}) copy-start(f32[640]{0:T(1024)} %param.13) | copy-start | bytes 7684
  23.8 33.7 %copy-start.10 = (s32[28]{0:T(128)S(1)}, s32[28]{0:T(128)}, u32[]{:S(2)}) copy-start(s32[28]{0:T(128)} %param.12) | copy-start | bytes 340
  51.9 6.6 %collective-permute-start = (bf16[8,1,16,640]{3,2,1,0:T(8,128)(2,1)S(1)}, bf16[8,1,16,640]{3,2,1,0:T(8,128)(2,1)S(1)}, u32[]{:S(2)}, u32[]{:S(2)}) collective-permute-start(bf16[8,1,16,640]{3,2,1,0:T(8,128)(2,1)S(1)} %fusion.38), channel_id=1, source_target_pairs={{0,1},{1,2},{2,3},{3,4},{4,5},{5,6},{6,7},{8,9},{9,10},{10,11},{11... | collective-permute-start | bytes 491528 | tf_op jit(solution)/shard_map/ppermute | solution.py:27
  53.8 6.5 %collective-permute-start.1 = (bf16[8,1,16,640]{3,2,1,0:T(8,128)(2,1)S(1)}, bf16[8,1,16,640]{3,2,1,0:T(8,128)(2,1)S(1)}, u32[]{:S(2)}, u32[]{:S(2)}) collective-permute-start(bf16[8,1,16,640]{3,2,1,0:T(8,128)(2,1)S(1)} %fusion.38), channel_id=1, source_target_pairs={{1,0},{2,1},{3,2},{4,3},{5,4},{6,5},{7,6},{9,8},{10,9},{11,10},{12... | collective-permute-start | bytes 491528 | tf_op jit(solution)/shard_map/ppermute | solution.py:29
  60.6 60.5 %copy-start.6 = (f32[640]{0:T(1024)S(1)}, f32[640]{0:T(1024)}, u32[]{:S(2)}) copy-start(f32[640]{0:T(1024)} %param.16) | copy-start | bytes 7684
  121.0 5.3 %copy-start.7 = (f32[640]{0:T(1024)S(1)}, f32[640]{0:T(1024)}, u32[]{:S(2)}) copy-start(f32[640]{0:T(1024)} %param.18) | copy-start | bytes 7684
  121.0 5.3 %copy-start.8 = (f32[640]{0:T(1024)S(1)}, f32[640]{0:T(1024)}, u32[]{:S(2)}) copy-start(f32[640]{0:T(1024)} %param.17) | copy-start | bytes 7684
  127.1 16.6 %collective-permute-start.6 = (bf16[8,16,640]{2,1,0:T(8,128)(2,1)S(1)}, bf16[8,16,640]{2,1,0:T(8,128)(2,1)S(1)}, u32[]{:S(2)}, u32[]{:S(2)}) collective-permute-start(bf16[8,16,640]{2,1,0:T(8,128)(2,1)S(1)} %get-tuple-element.11), channel_id=1, source_target_pairs={{0,16},{8,24},{16,32},{24,40},{32,48},{40,56},{48,64},{56,72},{64,... | collective-permute-start | bytes 491528 | tf_op jit(solution)/shard_map/ppermute | solution.py:16
  129.8 15.2 %collective-permute-start.2 = (bf16[8,16,640]{2,1,0:T(8,128)(2,1)S(1)}, bf16[8,16,640]{2,1,0:T(8,128)(2,1)S(1)}, u32[]{:S(2)}, u32[]{:S(2)}) collective-permute-start(bf16[8,16,640]{2,1,0:T(8,128)(2,1)S(1)} %get-tuple-element.10), channel_id=1, source_target_pairs={{0,16},{8,24},{16,32},{24,40},{32,48},{40,56},{48,64},{56,72},{64,... | collective-permute-start | bytes 491528 | tf_op jit(solution)/shard_map/ppermute | solution.py:16
  134.8 12.2 %collective-permute-start.7 = (bf16[8,16,640]{2,1,0:T(8,128)(2,1)S(1)}, bf16[8,16,640]{2,1,0:T(8,128)(2,1)S(1)}, u32[]{:S(2)}, u32[]{:S(2)}) collective-permute-start(bf16[8,16,640]{2,1,0:T(8,128)(2,1)S(1)} %get-tuple-element.11), channel_id=1, source_target_pairs={{0,8},{8,16},{16,24},{24,32},{32,40},{40,48},{48,56},{56,64},{64,7... | collective-permute-start | bytes 491528 | tf_op jit(solution)/shard_map/ppermute | solution.py:16
  138.6 9.7 %collective-permute-start.3 = (bf16[8,16,640]{2,1,0:T(8,128)(2,1)S(1)}, bf16[8,16,640]{2,1,0:T(8,128)(2,1)S(1)}, u32[]{:S(2)}, u32[]{:S(2)}) collective-permute-start(bf16[8,16,640]{2,1,0:T(8,128)(2,1)S(1)} %get-tuple-element.10), channel_id=1, source_target_pairs={{0,8},{8,16},{16,24},{24,32},{32,40},{40,48},{48,56},{56,64},{64,7... | collective-permute-start | bytes 491528 | tf_op jit(solution)/shard_map/ppermute | solution.py:16
  142.4 9.1 %collective-permute-start.4 = (bf16[8,16,640]{2,1,0:T(8,128)(2,1)S(1)}, bf16[8,16,640]{2,1,0:T(8,128)(2,1)S(1)}, u32[]{:S(2)}, u32[]{:S(2)}) collective-permute-start(bf16[8,16,640]{2,1,0:T(8,128)(2,1)S(1)} %get-tuple-element.10), channel_id=1, source_target_pairs={{8,0},{16,8},{24,16},{32,24},{40,32},{48,40},{56,48},{64,56},{72,6... | collective-permute-start | bytes 491528 | tf_op jit(solution)/shard_map/ppermute | solution.py:16
  143.7 16.5 %collective-permute-start.5 = (bf16[8,16,640]{2,1,0:T(8,128)(2,1)S(1)}, bf16[8,16,640]{2,1,0:T(8,128)(2,1)S(1)}, u32[]{:S(2)}, u32[]{:S(2)}) collective-permute-start(bf16[8,16,640]{2,1,0:T(8,128)(2,1)S(1)} %get-tuple-element.10), channel_id=1, source_target_pairs={{16,0},{24,8},{32,16},{40,24},{48,32},{56,40},{64,48},{72,56},{80,... | collective-permute-start | bytes 491528 | tf_op jit(solution)/shard_map/ppermute | solution.py:16
  145.0 19.9 %collective-permute-start.8 = (bf16[8,16,640]{2,1,0:T(8,128)(2,1)S(1)}, bf16[8,16,640]{2,1,0:T(8,128)(2,1)S(1)}, u32[]{:S(2)}, u32[]{:S(2)}) collective-permute-start(bf16[8,16,640]{2,1,0:T(8,128)(2,1)S(1)} %get-tuple-element.11), channel_id=1, source_target_pairs={{8,0},{16,8},{24,16},{32,24},{40,32},{48,40},{56,48},{64,56},{72,6... | collective-permute-start | bytes 491528 | tf_op jit(solution)/shard_map/ppermute | solution.py:16
  147.0 21.3 %collective-permute-start.9 = (bf16[8,16,640]{2,1,0:T(8,128)(2,1)S(1)}, bf16[8,16,640]{2,1,0:T(8,128)(2,1)S(1)}, u32[]{:S(2)}, u32[]{:S(2)}) collective-permute-start(bf16[8,16,640]{2,1,0:T(8,128)(2,1)S(1)} %get-tuple-element.11), channel_id=1, source_target_pairs={{16,0},{24,8},{32,16},{40,24},{48,32},{56,40},{64,48},{72,56},{80,... | collective-permute-start | bytes 491528 | tf_op jit(solution)/shard_map/ppermute | solution.py:16
  149.7 0.9 copy-start.3
  176.3 1.8 copy-start.2
  178.0 1.5 copy-start.9
Sparse Core Ops, SparseCore 0:
  23.9 97.0 all-gather.2
